TPU v7x, 32 devices: a whole 2x2x4 slice. The times are simulated.
32 devices in a mesh: bank: 2 (over x), basis: 16 (over z, y, core).
Axes of the slice: x: 2, y: 2, z: 4, core: 2. Of those that a mesh axis runs over, the one named last changes fastest.
Arguments:
- strain: float32 [256, 4, 2, 128], P('basis'), may hold values from -6 to 6
- basis_vectors: bfloat16 [64, 256, 2, 128], P(('bank', 'basis')), parts along dimension 0, may hold values from -0.0234375 to 0.0234375
- coefficients: float32 [512, 2, 32], P(('bank', 'basis')), parts along dimension 0, may hold values from -0.75 to 0.75
- template_rows: int32 [512], P('bank'), parts along dimension 0, may hold values from 0 to 255
Outputs:
- snr_power: float32 [4, 512, 256, 256], P(None, 'bank', 'basis'), parts along dimension 1
There are 2 independent parts, one for each index of `bank`. A program takes and returns all parts, laid end to end along the dimension named above; an argument that names none is the same for every part. Nothing has to cross between parts.
Inputs may be any that keep to these rules, and one draw needn't show every extreme that they name: template_rows[j] is the coefficient row of the j-th of the 256 rebuilt templates, the same for every sample.
All inputs are finite; a program needn't handle non-finite values.
Results may differ from a plain program's by a relative error of at most 0.0041.
Values may be sent and summed in bfloat16 or wider, within the bound.
A program may use at most 192 MiB of HBM per device.

v0:
```python
import functools
import math

import jax
import jax.numpy as jnp
import numpy as np
from jax import lax
from jax.experimental import pallas as pl
from jax.experimental.pallas import tpu as pltpu
from jax.sharding import PartitionSpec as P

highest = lax.Precision.HIGHEST


def rotation(left_index, right_index, period):
    turns = left_index * right_index % period
    angle = turns.astype(jnp.float32) * (2.0 * math.pi / period)
    return (jnp.cos(angle), jnp.sin(angle))


def complex_einsum(form, left_re, left_im, right_re, right_im):
    real_out = jnp.einsum(form, left_re, right_re, precision=highest) - jnp.einsum(
        form, left_im, right_im, precision=highest
    )
    imag_out = jnp.einsum(form, left_re, right_im, precision=highest) + jnp.einsum(
        form, left_im, right_re, precision=highest
    )
    return (real_out, imag_out)


def stack_rows(coeff_table, template_rows):
    chosen = coeff_table[template_rows].astype(jnp.bfloat16)
    return jnp.concatenate([chosen[:, 0], chosen[:, 1]], axis=0)


def rebuild(stacked, series_re, series_im):
    templates = stacked.shape[0] // 2
    left_sum = jnp.einsum("jk,sktu->sjtu", stacked, series_re, preferred_element_type=jnp.float32)
    right_sum = jnp.einsum("jk,sktu->sjtu", stacked, series_im, preferred_element_type=jnp.float32)
    rho_re = left_sum[:, :templates] - right_sum[:, templates:]
    rho_im = right_sum[:, :templates] + left_sum[:, templates:]
    return rho_re * rho_re + rho_im * rho_im


def shards_general(strain, basis_vectors, coefficients, template_rows):
    half_rows = strain.shape[3]
    side_len = 2 * half_rows
    samples = side_len * side_len
    freq_index = lax.broadcasted_iota(jnp.int32, (half_rows, side_len), 0)
    time_index = lax.broadcasted_iota(jnp.int32, (half_rows, side_len), 1)
    first_cos, first_sin = rotation(freq_index, time_index, side_len)
    column_index = lax.broadcasted_iota(jnp.int32, (side_len, side_len), 0)
    block_index = lax.broadcasted_iota(jnp.int32, (side_len, side_len), 1)
    second_cos, second_sin = rotation(column_index, block_index, side_len)
    coeff_table, whole_strain = (
        lax.all_gather(coefficients, "basis", axis=0, tiled=True),
        lax.all_gather(strain, "basis", axis=0, tiled=True),
    )
    stacked = stack_rows(coeff_table, template_rows)
    widened = basis_vectors.astype(jnp.float32)
    basis_re = widened[:, :, 0][None]
    basis_im = widened[:, :, 1][None]
    strain_re = jnp.transpose(whole_strain[:, :, 0], (1, 0, 2))[:, None]
    strain_im = jnp.transpose(whole_strain[:, :, 1], (1, 0, 2))[:, None]
    prod_re = basis_re * strain_re + basis_im * strain_im
    prod_im = basis_re * strain_im - basis_im * strain_re
    section_re, section_im = complex_einsum("skcr,rt->skct", prod_re, prod_im, first_cos, first_sin)
    twist_cos, twist_sin = rotation(column_index, block_index, samples)
    turned_re = section_re * twist_cos - section_im * twist_sin
    turned_im = section_re * twist_sin + section_im * twist_cos
    series_re, series_im = complex_einsum(
        "skct,cu->sktu", turned_re, turned_im, second_cos, second_sin
    )
    series_re = series_re.astype(jnp.bfloat16)
    series_im = series_im.astype(jnp.bfloat16)
    return rebuild(
        stacked,
        lax.all_to_all(series_re, "basis", split_axis=2, concat_axis=1, tiled=True),
        lax.all_to_all(series_im, "basis", split_axis=2, concat_axis=1, tiled=True),
    )


bf16 = jnp.bfloat16
f32 = jnp.float32
NT = (((1,), (1,)), ((), ()))
TN = (((0,), (0,)), ((), ()))


def split(values):
    high = values.astype(bf16)
    return high, (values - high.astype(f32)).astype(bf16)


def table(rows, columns, period):
    turns = np.outer(np.arange(rows), np.arange(columns)) % period
    angle = turns * (2.0 * math.pi / period)
    return np.cos(angle), np.sin(angle)


def halves(values):
    values = values.astype(np.float32)
    high = values.astype(bf16)
    return high, (values - high.astype(np.float32)).astype(bf16)


def exchange(n, segs, u_ref, strain_ref, coeff_ref, first_hi, first_lo, turn_ref, got_ref, table_ref,
             u_all, wide_re, wide_im, sect, packed, send_u, recv_u, send_c, recv_c, send_s, recv_s, own_sem):
    me = lax.axis_index("basis")
    cols = u_ref.shape[1] // n
    k_loc = u_ref.shape[0]
    side = u_ref.shape[1]
    half = side // 2
    n_k = k_loc * n
    res = side // n

    barrier = pltpu.get_barrier_semaphore()
    for off in range(1, n):
        pl.semaphore_signal(barrier, inc=1, device_id={"basis": lax.rem(me + off, n)},
                            device_id_type=pl.DeviceIdType.MESH)
    pl.semaphore_wait(barrier, n - 1)

    sends = []
    for off in range(1, n):
        peer = lax.rem(me + off, n)
        block = pl.ds(pl.multiple_of(peer * cols, cols), cols)
        sends.append(pltpu.make_async_remote_copy(
            u_ref.at[:, block], u_all.at[me], send_u.at[off], recv_u.at[off],
            device_id={"basis": peer}, device_id_type=pl.DeviceIdType.MESH))
        sends[-1].start()
    coeffs = []
    for off in range(1, n):
        peer = lax.rem(me + off, n)
        coeffs.append(pltpu.make_async_remote_copy(
            coeff_ref, table_ref.at[me], send_c.at[off], recv_c.at[off],
            device_id={"basis": peer}, device_id_type=pl.DeviceIdType.MESH))
        coeffs[-1].start()
    own_block = pl.ds(pl.multiple_of(me * cols, cols), cols)
    own_u = pltpu.make_async_copy(u_ref.at[:, own_block], u_all.at[me], own_sem.at[0])
    own_u.start()
    own_c = pltpu.make_async_copy(coeff_ref, table_ref.at[me], own_sem.at[1])
    own_c.start()
    own_u.wait()
    for copy in sends:
        copy.wait()

    wide = u_all[...].astype(f32).reshape(n_k * cols, side)
    wide_re[...] = wide[:, :half]
    wide_im[...] = wide[:, half:]
    for c in range(cols):
        u_re = wide_re[pl.ds(c, n_k, stride=cols), :]
        u_im = wide_im[pl.ds(c, n_k, stride=cols), :]
        parts = []
        for s in range(segs):
            row = c * segs + s
            d_re = strain_ref[row:row + 1, :half]
            d_im = strain_ref[row:row + 1, half:]
            parts.append(jnp.concatenate([u_re * d_re + u_im * d_im, u_re * d_im - u_im * d_re], axis=1))
        high, low = split(jnp.concatenate(parts, axis=0))
        out = lax.dot_general(first_hi[...], high, NT, preferred_element_type=f32)
        out += lax.dot_general(first_lo[...], high, NT, preferred_element_type=f32)
        out += lax.dot_general(first_hi[...], low, NT, preferred_element_type=f32)
        t_cos = turn_ref[:, c:c + 1]
        t_sin = turn_ref[:, cols + c:cols + c + 1]
        o_re, o_im = out[:side], out[side:]
        sect[0, pl.ds(c, side, stride=cols), :] = o_re * t_cos - o_im * t_sin
        sect[1, pl.ds(c, side, stride=cols), :] = o_re * t_sin + o_im * t_cos
    packed[...] = sect[...].astype(bf16).reshape(packed.shape)

    blocks = []
    for off in range(1, n):
        peer = lax.rem(me + off, n)
        blocks.append(pltpu.make_async_remote_copy(
            packed.at[:, pl.ds(peer * res, res)], got_ref.at[me], send_s.at[off], recv_s.at[off],
            device_id={"basis": peer}, device_id_type=pl.DeviceIdType.MESH))
        blocks[-1].start()
    own_s = pltpu.make_async_copy(packed.at[:, pl.ds(me * res, res)], got_ref.at[me], own_sem.at[2])
    own_s.start()
    own_c.wait()
    for copy in coeffs:
        copy.wait()
    own_s.wait()
    for copy in blocks:
        copy.wait()


def rebuild_kernel(segs, got_ref, table_ref, rows_ref, second_hi, second_lo, out_ref,
                   series, left_re, left_im, stage, out_sem):
    n, _, res, cols, wide = got_ref.shape
    side = n * cols
    n_k = wide // segs
    step_s = pl.program_id(0)
    step_j = pl.program_id(1)
    j_steps = pl.num_programs(1)
    j_block = out_ref.shape[1] // res // j_steps
    step = step_s * j_steps + step_j
    slot = lax.rem(step, 2)

    def writes(at_slot, at_s, at_j):
        height = j_block * res
        span = pl.ds(pl.multiple_of(at_j * height, height), height)
        return [pltpu.make_async_copy(stage.at[at_slot, h], out_ref.at[at_s, span, pl.ds(h * 128, 128)],
                                      out_sem.at[at_slot, h]) for h in range(side // 128)]

    @pl.when((step_s == 0) & (step_j == 0))
    def _():
        n_rows = table_ref.shape[0]
        lanes = lax.broadcasted_iota(jnp.int32, (rows_ref.shape[0], n_rows), 1)
        hot = jnp.where(lanes == rows_ref[...], 1.0, 0.0).astype(bf16)
        left = jnp.dot(hot, table_ref[...], preferred_element_type=f32).astype(bf16)
        left_re[...] = left[:, :2 * n_k]
        left_im[...] = left[:, 2 * n_k:]

        @pl.loop(0, res)
        def _(a):
            both = []
            for part in range(2):
                block = got_ref[:, part, a].reshape(side, wide)
                both.append(lax.dot_general(block, second_hi[...], TN, preferred_element_type=f32)
                            + lax.dot_general(block, second_lo[...], TN, preferred_element_type=f32))
            z_re = (both[0][:, :side] - both[1][:, side:]).astype(bf16)
            z_im = (both[0][:, side:] + both[1][:, :side]).astype(bf16)
            for s in range(segs):
                series[s, a, :n_k] = z_re[s * n_k:(s + 1) * n_k]
                series[s, a, n_k:] = z_im[s * n_k:(s + 1) * n_k]

    @pl.when(step >= 2)
    def _():
        for copy in writes(slot, 0, 0):
            copy.wait()

    rows = pl.ds(pl.multiple_of(step_j * j_block, j_block), j_block)
    l_re = left_re[rows, :]
    l_im = left_im[rows, :]
    for a in range(res):
        right = series[step_s, a]
        p_re = jnp.dot(l_re, right, preferred_element_type=f32)
        p_im = jnp.dot(l_im, right, preferred_element_type=f32)
        power = p_re * p_re + p_im * p_im
        for h in range(side // 128):
            stage[slot, h, pl.ds(a, j_block, stride=res), :] = power[:, h * 128:(h + 1) * 128]
    for copy in writes(slot, step_s, step_j):
        copy.start()

    @pl.when(step == pl.num_programs(0) * j_steps - 1)
    def _():
        for at_slot in range(2):
            for copy in writes(at_slot, 0, 0):
                copy.wait()


def shards(n, strain, basis_vectors, coefficients, template_rows):
    cols, segs, _, half = strain.shape
    side = 2 * half
    k_loc = basis_vectors.shape[0]
    n_k = k_loc * n
    res = side // n
    templates = template_rows.shape[0]
    wide = segs * n_k
    if cols % 16 or wide != 128 or n_k % 16 or coefficients.shape[0] % 16:
        return shards_general(strain, basis_vectors, coefficients, template_rows)
    samples = side * side
    cos1, sin1 = table(side, half, side)
    first_hi, first_lo = halves(np.block([[cos1, -sin1], [sin1, cos1]]))
    cos2, sin2 = table(side, side, side)
    second_hi, second_lo = halves(np.concatenate([cos2, sin2], axis=1))
    me = lax.axis_index("basis")
    column = me * cols + lax.broadcasted_iota(jnp.int32, (side, cols), 1)
    turns = column * lax.broadcasted_iota(jnp.int32, (side, cols), 0) % samples
    angle = turns.astype(f32) * (2.0 * math.pi / samples)
    turn = jnp.concatenate([jnp.cos(angle), jnp.sin(angle)], axis=1)
    c_re, c_im = coefficients[:, 0].astype(bf16), coefficients[:, 1].astype(bf16)
    packed_coeff = jnp.concatenate([c_re, -c_im, c_im, c_re], axis=1)
    rows_loc = coefficients.shape[0]
    u = basis_vectors.reshape(k_loc, side, side)
    d = strain.reshape(cols * segs, side)
    vmem = pl.BlockSpec(memory_space=pltpu.VMEM)
    hbm = pl.BlockSpec(memory_space=pl.ANY)
    got, coeff_table = pl.pallas_call(
        functools.partial(exchange, n, segs),
        out_shape=[jax.ShapeDtypeStruct((n, 2, res, cols, wide), bf16),
                   jax.ShapeDtypeStruct((n, rows_loc, 4 * n_k), bf16)],
        in_specs=[vmem] * 6,
        out_specs=[hbm, hbm],
        scratch_shapes=[
            pltpu.VMEM((n, k_loc, cols, side), bf16),
            pltpu.VMEM((n_k * cols, half), f32),
            pltpu.VMEM((n_k * cols, half), f32),
            pltpu.VMEM((2, side * cols, wide), f32),
            pltpu.VMEM((2, side, cols, wide), bf16),
        ] + [pltpu.SemaphoreType.DMA((n,))] * 6 + [pltpu.SemaphoreType.DMA((3,))],
        compiler_params=pltpu.CompilerParams(collective_id=0, has_side_effects=True),
    )(u, d, packed_coeff, first_hi, first_lo, turn)
    j_block = templates // 2
    power = pl.pallas_call(
        functools.partial(rebuild_kernel, segs),
        grid=(segs, templates // j_block),
        out_shape=jax.ShapeDtypeStruct((segs, templates * res, side), f32),
        in_specs=[vmem] * 5,
        out_specs=hbm,
        scratch_shapes=[
            pltpu.VMEM((segs, res, 2 * n_k, side), bf16),
            pltpu.VMEM((templates, 2 * n_k), bf16),
            pltpu.VMEM((templates, 2 * n_k), bf16),
            pltpu.VMEM((2, side // 128, j_block * res, 128), f32),
            pltpu.SemaphoreType.DMA((2, side // 128)),
        ],
    )(got, coeff_table.reshape(n * rows_loc, 4 * n_k), template_rows[:, None], second_hi, second_lo)
    return power.reshape(segs, templates, res, side)


def solution(mesh):
    in_specs = (
        P("basis", None, None, None),
        P(("bank", "basis"), None, None, None),
        P(("bank", "basis"), None, None),
        P("bank"),
    )
    out_specs = P(None, "bank", "basis", None)
    return jax.shard_map(functools.partial(shards, mesh.shape["basis"]), mesh=mesh, in_specs=in_specs, out_specs=out_specs, check_vma=False)
```

profile of v0, /device:TPU:29, one launch (start us, length us, event | category | flops | bytes accessed | tf_op | source)
XLA Modules:
  0.0 91.3 jit_solution(1531658845992269370)
XLA Ops:
  0.0 0.7 copy.18
  0.7 0.7 pad_maximum_fusion.1.coeff_ref
  1.4 0.2 fusion.7
  1.6 1.5 %copy.19 = f32[8,8,2,128]{3,1,2,0:T(8,128)} copy(f32[8,8,2,128]{3,2,1,0:T(2,128)} %bitcast.16) | data formatting | bytes 131072
  3.0 0.8 copy.13.turn_ref
  3.8 1.5 %copy.14.rows_ref = s32[256,1]{1,0:T(8,128)} copy(s32[256,1]{0,1:T(1,128)} %bitcast.17) | data formatting | bytes 2048 | tf_op jit(solution)/shard_map/broadcast_in_dim | solution.py:307
  5.3 1.8 %reshape.14.u_ref = bf16[2,256,256]{2,1,0:T(8,128)(2,1)} reshape(bf16[2,256,2,128]{3,2,1,0:T(2,128)(2,1)} %param.9) | data formatting | bytes 524288 | tf_op jit(solution)/shard_map/reshape | solution.py:274
  7.1 64.7 %shard_map.82 = (bf16[16,2,16,16,128]{4,3,2,1,0:T(8,128)(2,1)}, bf16[16,16,128]{2,1,0:T(8,128)(2,1)}) custom-call(bf16[2,256,256]{2,1,0:T(8,128)(2,1)} %reshape.14.u_ref, f32[64,256]{1,0:T(8,128)} %bitcast.14, bf16[16,128]{1,0:T(8,128)(2,1)} %pad_maximum_fusion.1.coeff_ref, bf16[512,256]{1,0:T(8,128)(2,1)} %constant.31.clone.first_hi, ...), custom_call_target="tpu_custom_call" | custom-call | tf_op jit(solution)/shard_map/pallas_call | solution.py:278
  71.8 19.5 %shard_map.83 = f32[4,4096,256]{2,1,0:T(8,128)} custom-call(bf16[16,2,16,16,128]{4,3,2,1,0:T(8,128)(2,1)} %get-tuple-element.7.got_ref, bf16[256,128]{1,0:T(8,128)(2,1)} %bitcast.15, s32[256,1]{1,0:T(8,128)} %copy.14.rows_ref, bf16[256,512]{1,0:T(8,128)(2,1)} %constant.33.clone.second_hi, bf16[256,512]{1,0:T(8,128)(2,1)} %constant.34.clone.second_lo), custom_call_target="tpu_custom_call" | custom-call | tf_op jit(solution)/shard_map/pallas_call | solution.py:294
  (4 shorter events, 0.0 us)
where the time goes:
time: 91.6 us; the launch traced here: 91.3 us
  Pallas kernels  84.2 us (92%)
  local copies, waits for them, and re-layouts  6.25 us (7%)
    pallas_call x1, Pallas kernels, shards(): pl.pallas_call(functools.partial(exchange, n, segs), out_shape=[jax.Shape...  64.7 us
    pallas_call x1, Pallas kernels, shards(): pl.pallas_call(functools.partial(rebuild_kernel, segs), grid=(segs, templ...  19.5 us
    unnamed x2, local copies, waits for them, and re-layouts  2.19 us

commit v1 on v0

--- a/solution.py
+++ b/solution.py
@@ -103,84 +103,168 @@
     return high, (values - high.astype(np.float32)).astype(bf16)
 
 
-def exchange(n, segs, u_ref, strain_ref, coeff_ref, first_hi, first_lo, turn_ref, got_ref, table_ref,
-             u_all, wide_re, wide_im, sect, packed, send_u, recv_u, send_c, recv_c, send_s, recv_s, own_sem):
+def exchange(n, group, segs, u_ref, strain_ref, coeff_ref, first_hi, first_lo, turn_ref, got_ref, table_ref,
+             u_all, strain_all, wide_re, wide_im, sect, packed, left_hi, left_lo,
+             send_u, recv_u, send_z, recv_z, send_d, recv_d, send_c, recv_c, send_s, recv_s, own_sem):
     me = lax.axis_index("basis")
-    cols = u_ref.shape[1] // n
-    k_loc = u_ref.shape[0]
-    side = u_ref.shape[1]
+    layers = n // group
+    layer = me // group
+    lane = lax.rem(me, group)
+    k_loc, side = u_ref.shape[0], u_ref.shape[1]
+    cols = side // n
     half = side // 2
     n_k = k_loc * n
     res = side // n
+    near = group * res
+
+    def remote(src, dst, send, recv, peer):
+        return pltpu.make_async_remote_copy(src, dst, send, recv, device_id={"basis": peer},
+                                            device_id_type=pl.DeviceIdType.MESH)
+
+    def mate(off):
+        return lax.rem(lane + off, group)
+
+    def columns(q, owner):
+        return pl.ds(pl.multiple_of((q * group + owner) * cols, cols), cols)
+
+    def swap_u(off, q):
+        to = mate(off)
+        return remote(u_ref.at[:, columns(q, to)], u_all.at[q, layer, lane], send_u.at[off, q], recv_u.at[off, q],
+                      layer * group + to)
+
+    def swap_s(off, q):
+        to = mate(off)
+        rows = pl.ds(pl.multiple_of(to * res, res), res)
+        return remote(packed.at[q, :, rows], got_ref.at[q * group + lane], send_s.at[off, q], recv_s.at[off, q],
+                      layer * group + to)
+
+    def keep_u(q):
+        return pltpu.make_async_copy(u_ref.at[:, columns(q, lane)], u_all.at[q, layer, lane], own_sem.at[0, q])
+
+    def keep_s(q):
+        rows = pl.ds(pl.multiple_of(lane * res, res), res)
+        return pltpu.make_async_copy(packed.at[q, :, rows], got_ref.at[q * group + lane], own_sem.at[1, q])
+
+    def pass_u(q, origin, way):
+        return remote(u_all.at[q, origin], u_all.at[q, origin], send_z.at[q, origin, way], recv_z.at[q, origin],
+                      me + (2 * way - 1) * group)
+
+    def pass_d(origin, way):
+        return remote(strain_all.at[origin], strain_all.at[origin], send_d.at[origin, way], recv_d.at[origin],
+                      me + (2 * way - 1) * group)
+
+    def share_c(off):
+        return remote(coeff_ref, table_ref.at[me], send_c.at[off], recv_c.at[off], lax.rem(me + off, n))
+
+    def towards(way):
+        return layer < layers - 1 if way else layer > 0
+
+    def relay(copy_of):
+        for dist in range(1, layers):
+            for way in range(2):
+                origin = layer - dist if way else layer + dist
+
+                @pl.when((origin >= 0) & (origin < layers))
+                def _():
+                    copy_of(origin, 0).wait_recv()
+
+                    @pl.when(towards(way))
+                    def _():
+                        copy_of(origin, way).start()
+
+    def drain(copy_of):
+        for origin in range(layers):
+            for way in range(2):
+                sent = origin <= layer if way else origin >= layer
+
+                @pl.when(towards(way) & sent)
+                def _():
+                    copy_of(origin, way).wait_send()
+
+    def launch(q):
+        keep_u(q).wait()
+        for off in range(1, group):
+            swap_u(off, q).wait_recv()
+        for way in range(2):
+            @pl.when(towards(way))
+            def _():
+                pass_u(q, layer, way).start()
 
     barrier = pltpu.get_barrier_semaphore()
     for off in range(1, n):
         pl.semaphore_signal(barrier, inc=1, device_id={"basis": lax.rem(me + off, n)},
                             device_id_type=pl.DeviceIdType.MESH)
+    own_d = pltpu.make_async_copy(strain_ref, strain_all.at[layer], own_sem.at[2, 0])
+    own_d.start()
+    own_c = pltpu.make_async_copy(coeff_ref, table_ref.at[me], own_sem.at[2, 1])
+    own_c.start()
+    for q in range(layers):
+        keep_u(q).start()
+    own_d.wait()
     pl.semaphore_wait(barrier, n - 1)
-
-    sends = []
+    for q in range(layers):
+        for off in range(1, group):
+            swap_u(off, q).start()
+    for way in range(2):
+        @pl.when(towards(way))
+        def _():
+            pass_d(layer, way).start()
     for off in range(1, n):
-        peer = lax.rem(me + off, n)
-        block = pl.ds(pl.multiple_of(peer * cols, cols), cols)
-        sends.append(pltpu.make_async_remote_copy(
-            u_ref.at[:, block], u_all.at[me], send_u.at[off], recv_u.at[off],
-            device_id={"basis": peer}, device_id_type=pl.DeviceIdType.MESH))
-        sends[-1].start()
-    coeffs = []
+        share_c(off).start()
+    for part in range(2):
+        rows = pl.ds(pl.multiple_of(part * side + layer * near, near), near)
+        left_hi[part * near:(part + 1) * near, :] = first_hi[rows, :]
+        left_lo[part * near:(part + 1) * near, :] = first_lo[rows, :]
+    launch(0)
+    relay(pass_d)
+    launch(1)
+
+    @pl.loop(0, layers)
+    def _(q):
+        relay(functools.partial(pass_u, q))
+
+        @pl.when(q + 2 < layers)
+        def _():
+            launch(q + 2)
+
+        wide = u_all[q].astype(f32).reshape(n_k * cols, side)
+        wide_re[...] = wide[:, :half]
+        wide_im[...] = wide[:, half:]
+        turn = turn_ref[q]
+        for c in range(cols):
+            u_re = wide_re[pl.ds(c, n_k, stride=cols), :]
+            u_im = wide_im[pl.ds(c, n_k, stride=cols), :]
+            parts = []
+            for s in range(segs):
+                d_row = strain_all[q, c * segs + s:c * segs + s + 1, :]
+                d_re, d_im = d_row[:, :half], d_row[:, half:]
+                parts.append(jnp.concatenate([u_re * d_re + u_im * d_im, u_re * d_im - u_im * d_re], axis=1))
+            high, low = split(jnp.concatenate(parts, axis=0))
+            out = lax.dot_general(left_hi[...], high, NT, preferred_element_type=f32)
+            out += lax.dot_general(left_lo[...], high, NT, preferred_element_type=f32)
+            out += lax.dot_general(left_hi[...], low, NT, preferred_element_type=f32)
+            t_cos = turn[:, c:c + 1]
+            t_sin = turn[:, cols + c:cols + c + 1]
+            o_re, o_im = out[:near], out[near:]
+            sect[0, pl.ds(c, near, stride=cols), :] = o_re * t_cos - o_im * t_sin
+            sect[1, pl.ds(c, near, stride=cols), :] = o_re * t_sin + o_im * t_cos
+        packed[q] = sect[...].astype(bf16).reshape(packed.shape[1:])
+        for off in range(1, group):
+            swap_s(off, q).start()
+        keep_s(q).start()
+
+    own_c.wait()
     for off in range(1, n):
-        peer = lax.rem(me + off, n)
-        coeffs.append(pltpu.make_async_remote_copy(
-            coeff_ref, table_ref.at[me], send_c.at[off], recv_c.at[off],
-            device_id={"basis": peer}, device_id_type=pl.DeviceIdType.MESH))
-        coeffs[-1].start()
-    own_block = pl.ds(pl.multiple_of(me * cols, cols), cols)
-    own_u = pltpu.make_async_copy(u_ref.at[:, own_block], u_all.at[me], own_sem.at[0])
-    own_u.start()
-    own_c = pltpu.make_async_copy(coeff_ref, table_ref.at[me], own_sem.at[1])
-    own_c.start()
-    own_u.wait()
-    for copy in sends:
-        copy.wait()
-
-    wide = u_all[...].astype(f32).reshape(n_k * cols, side)
-    wide_re[...] = wide[:, :half]
-    wide_im[...] = wide[:, half:]
-    for c in range(cols):
-        u_re = wide_re[pl.ds(c, n_k, stride=cols), :]
-        u_im = wide_im[pl.ds(c, n_k, stride=cols), :]
-        parts = []
-        for s in range(segs):
-            row = c * segs + s
-            d_re = strain_ref[row:row + 1, :half]
-            d_im = strain_ref[row:row + 1, half:]
-            parts.append(jnp.concatenate([u_re * d_re + u_im * d_im, u_re * d_im - u_im * d_re], axis=1))
-        high, low = split(jnp.concatenate(parts, axis=0))
-        out = lax.dot_general(first_hi[...], high, NT, preferred_element_type=f32)
-        out += lax.dot_general(first_lo[...], high, NT, preferred_element_type=f32)
-        out += lax.dot_general(first_hi[...], low, NT, preferred_element_type=f32)
-        t_cos = turn_ref[:, c:c + 1]
-        t_sin = turn_ref[:, cols + c:cols + c + 1]
-        o_re, o_im = out[:side], out[side:]
-        sect[0, pl.ds(c, side, stride=cols), :] = o_re * t_cos - o_im * t_sin
-        sect[1, pl.ds(c, side, stride=cols), :] = o_re * t_sin + o_im * t_cos
-    packed[...] = sect[...].astype(bf16).reshape(packed.shape)
-
-    blocks = []
-    for off in range(1, n):
-        peer = lax.rem(me + off, n)
-        blocks.append(pltpu.make_async_remote_copy(
-            packed.at[:, pl.ds(peer * res, res)], got_ref.at[me], send_s.at[off], recv_s.at[off],
-            device_id={"basis": peer}, device_id_type=pl.DeviceIdType.MESH))
-        blocks[-1].start()
-    own_s = pltpu.make_async_copy(packed.at[:, pl.ds(me * res, res)], got_ref.at[me], own_sem.at[2])
-    own_s.start()
-    own_c.wait()
-    for copy in coeffs:
-        copy.wait()
-    own_s.wait()
-    for copy in blocks:
-        copy.wait()
+        share_c(off).wait()
+    drain(pass_d)
+
+    @pl.loop(0, layers)
+    def _(q):
+        drain(functools.partial(pass_u, q))
+        keep_s(q).wait()
+        for off in range(1, group):
+            swap_u(off, q).wait_send()
+            swap_s(off, q).wait()
 
 
 def rebuild_kernel(segs, got_ref, table_ref, rows_ref, second_hi, second_lo, out_ref,
@@ -204,9 +288,9 @@
     @pl.when((step_s == 0) & (step_j == 0))
     def _():
         n_rows = table_ref.shape[0]
-        lanes = lax.broadcasted_iota(jnp.int32, (rows_ref.shape[0], n_rows), 1)
-        hot = jnp.where(lanes == rows_ref[...], 1.0, 0.0).astype(bf16)
-        left = jnp.dot(hot, table_ref[...], preferred_element_type=f32).astype(bf16)
+        index = lax.broadcasted_iota(jnp.int32, (n_rows, rows_ref.shape[1]), 0)
+        hot = jnp.where(index == rows_ref[...], 1.0, 0.0).astype(bf16)
+        left = lax.dot_general(hot, table_ref[...], TN, preferred_element_type=f32).astype(bf16)
         left_re[...] = left[:, :2 * n_k]
         left_im[...] = left[:, 2 * n_k:]
 
@@ -256,7 +340,7 @@
     res = side // n
     templates = template_rows.shape[0]
     wide = segs * n_k
-    if cols % 16 or wide != 128 or n_k % 16 or coefficients.shape[0] % 16:
+    if cols % 16 or wide != 128 or n_k % 16 or coefficients.shape[0] % 16 or math.isqrt(n) ** 2 != n:
         return shards_general(strain, basis_vectors, coefficients, template_rows)
     samples = side * side
     cos1, sin1 = table(side, half, side)
@@ -264,10 +348,14 @@
     cos2, sin2 = table(side, side, side)
     second_hi, second_lo = halves(np.concatenate([cos2, sin2], axis=1))
     me = lax.axis_index("basis")
-    column = me * cols + lax.broadcasted_iota(jnp.int32, (side, cols), 1)
-    turns = column * lax.broadcasted_iota(jnp.int32, (side, cols), 0) % samples
-    angle = turns.astype(f32) * (2.0 * math.pi / samples)
-    turn = jnp.concatenate([jnp.cos(angle), jnp.sin(angle)], axis=1)
+    group = math.isqrt(n)
+    layers = n // group
+    grid = (layers, group * res, cols)
+    lane = me % group
+    column = (lax.broadcasted_iota(jnp.int32, grid, 0) * group + lane) * cols + lax.broadcasted_iota(jnp.int32, grid, 2)
+    residue = me // group * group * res + lax.broadcasted_iota(jnp.int32, grid, 1)
+    angle = (column * residue % samples).astype(f32) * (2.0 * math.pi / samples)
+    turn = jnp.concatenate([jnp.cos(angle), jnp.sin(angle)], axis=2)
     c_re, c_im = coefficients[:, 0].astype(bf16), coefficients[:, 1].astype(bf16)
     packed_coeff = jnp.concatenate([c_re, -c_im, c_im, c_re], axis=1)
     rows_loc = coefficients.shape[0]
@@ -276,18 +364,23 @@
     vmem = pl.BlockSpec(memory_space=pltpu.VMEM)
     hbm = pl.BlockSpec(memory_space=pl.ANY)
     got, coeff_table = pl.pallas_call(
-        functools.partial(exchange, n, segs),
+        functools.partial(exchange, n, group, segs),
         out_shape=[jax.ShapeDtypeStruct((n, 2, res, cols, wide), bf16),
                    jax.ShapeDtypeStruct((n, rows_loc, 4 * n_k), bf16)],
         in_specs=[vmem] * 6,
         out_specs=[hbm, hbm],
         scratch_shapes=[
-            pltpu.VMEM((n, k_loc, cols, side), bf16),
+            pltpu.VMEM((layers, layers, group, k_loc, cols, side), bf16),
+            pltpu.VMEM((layers, cols * segs, side), f32),
             pltpu.VMEM((n_k * cols, half), f32),
             pltpu.VMEM((n_k * cols, half), f32),
-            pltpu.VMEM((2, side * cols, wide), f32),
-            pltpu.VMEM((2, side, cols, wide), bf16),
-        ] + [pltpu.SemaphoreType.DMA((n,))] * 6 + [pltpu.SemaphoreType.DMA((3,))],
+            pltpu.VMEM((2, group * res * cols, wide), f32),
+            pltpu.VMEM((layers, 2, group * res, cols, wide), bf16),
+            pltpu.VMEM((2 * group * res, side), bf16),
+            pltpu.VMEM((2 * group * res, side), bf16),
+        ] + [pltpu.SemaphoreType.DMA(dims) for dims in (
+            (group, layers), (group, layers), (layers, layers, 2), (layers, layers), (layers, 2), (layers,),
+            (n,), (n,), (group, layers), (group, layers), (3, layers))],
         compiler_params=pltpu.CompilerParams(collective_id=0, has_side_effects=True),
     )(u, d, packed_coeff, first_hi, first_lo, turn)
     j_block = templates // 2
@@ -304,7 +397,7 @@
             pltpu.VMEM((2, side // 128, j_block * res, 128), f32),
             pltpu.SemaphoreType.DMA((2, side // 128)),
         ],
-    )(got, coeff_table.reshape(n * rows_loc, 4 * n_k), template_rows[:, None], second_hi, second_lo)
+    )(got, coeff_table.reshape(n * rows_loc, 4 * n_k), template_rows[None], second_hi, second_lo)
     return power.reshape(segs, templates, res, side)
 
 

time: 91.6 us -> 74.1 us (0.81)
  the two profiles are of different devices: /device:TPU:29 before, /device:TPU:1 now
where the time goes in v1:
time: 74.1 us; the launch traced here: 73.8 us
  Pallas kernels  67.6 us (91%)
  local copies, waits for them, and re-layouts  4.11 us (6%)
  other arithmetic  2 us (3%)
    pallas_call x1, Pallas kernels, shards(): pl.pallas_call(functools.partial(exchange, n, group, segs), out_shape=[ja...  48.2 us
    pallas_call x1, Pallas kernels, shards(): pl.pallas_call(functools.partial(rebuild_kernel, segs), grid=(segs, templ...  19.5 us
    unnamed x2, local copies, waits for them, and re-layouts  2.2 us
    reshape x1, local copies, waits for them, and re-layouts, shards(): u = basis_vectors.reshape(k_loc, side, side)  1.82 us

profile of v1, /device:TPU:1, one launch (start us, length us, event | category | flops | bytes accessed | tf_op | source)
XLA Modules:
  0.0 73.8 jit_solution(10267505515075693880)
XLA Ops:
  0.0 0.7 copy.15
  0.7 0.7 pad_maximum_fusion.1.coeff_ref
  1.4 0.1 fusion.1
  1.5 1.5 %copy.16 = f32[8,8,2,128]{3,1,2,0:T(8,128)} copy(f32[8,8,2,128]{3,2,1,0:T(2,128)} %bitcast.16) | data formatting | bytes 131072
  3.0 0.1 copy.11
  3.1 0.5 multiply_cosine_fusion
  3.5 0.8 %pad_maximum_fusion.turn_ref = f32[4,64,32]{2,1,0:T(8,128)} fusion(f32[4,64,16]{2,1,0:T(8,128)S(1)} %get-tuple-element.10, f32[4,64,16]{2,1,0:T(8,128)S(1)} %get-tuple-element.9), kind=kLoop, calls=%fused_computation | loop fusion | flops 8192 | bytes 65536 | tf_op jit(solution)/shard_map/concatenate | solution.py:358
  4.3 1.8 %reshape.14.u_ref = bf16[2,256,256]{2,1,0:T(8,128)(2,1)} reshape(bf16[2,256,2,128]{3,2,1,0:T(2,128)(2,1)} %param.9) | data formatting | bytes 524288 | tf_op jit(solution)/shard_map/reshape | solution.py:362
  6.1 48.2 %shard_map.82 = (bf16[16,2,16,16,128]{4,3,2,1,0:T(8,128)(2,1)}, bf16[16,16,128]{2,1,0:T(8,128)(2,1)}) custom-call(bf16[2,256,256]{2,1,0:T(8,128)(2,1)} %reshape.14.u_ref, f32[64,256]{1,0:T(8,128)} %bitcast.14, bf16[16,128]{1,0:T(8,128)(2,1)} %pad_maximum_fusion.1.coeff_ref, bf16[512,256]{1,0:T(8,128)(2,1)} %constant.60.clone.first_hi, ...), custom_call_target="tpu_custom_call" | custom-call | tf_op jit(solution)/shard_map/pallas_call | solution.py:366
  54.3 19.5 %shard_map.83 = f32[4,4096,256]{2,1,0:T(8,128)} custom-call(bf16[16,2,16,16,128]{4,3,2,1,0:T(8,128)(2,1)} %get-tuple-element.7.got_ref, bf16[256,128]{1,0:T(8,128)(2,1)} %bitcast.15, s32[1,256]{1,0:T(1,128)} %bitcast.17, bf16[256,512]{1,0:T(8,128)(2,1)} %constant.62.clone.second_hi, bf16[256,512]{1,0:T(8,128)(2,1)} %constant.63.clone.second_lo), custom_call_target="tpu_custom_call" | custom-call | tf_op jit(solution)/shard_map/pallas_call | solution.py:387
  (4 shorter events, 0.0 us)

commit v2 on v1

--- a/solution.py
+++ b/solution.py
@@ -186,6 +186,10 @@
         for off in range(1, group):
             swap_u(off, q).wait_recv()
         for way in range(2):
+            @pl.when(towards(way) & (layer == q))
+            def _():
+                pass_d(layer, way).start()
+
             @pl.when(towards(way))
             def _():
                 pass_u(q, layer, way).start()
@@ -205,22 +209,27 @@
     for q in range(layers):
         for off in range(1, group):
             swap_u(off, q).start()
-    for way in range(2):
-        @pl.when(towards(way))
-        def _():
-            pass_d(layer, way).start()
-    for off in range(1, n):
-        share_c(off).start()
     for part in range(2):
         rows = pl.ds(pl.multiple_of(part * side + layer * near, near), near)
         left_hi[part * near:(part + 1) * near, :] = first_hi[rows, :]
         left_lo[part * near:(part + 1) * near, :] = first_lo[rows, :]
     launch(0)
-    relay(pass_d)
+    for off in range(1, n):
+        share_c(off).start()
     launch(1)
 
     @pl.loop(0, layers)
     def _(q):
+        @pl.when(layer != q)
+        def _():
+            pass_d(q, 0).wait_recv()
+            for way in range(2):
+                ahead = layer > q if way else layer < q
+
+                @pl.when(towards(way) & ahead)
+                def _():
+                    pass_d(q, way).start()
+
         relay(functools.partial(pass_u, q))
 
         @pl.when(q + 2 < layers)
@@ -231,13 +240,14 @@
         wide_re[...] = wide[:, :half]
         wide_im[...] = wide[:, half:]
         turn = turn_ref[q]
+        strain_q = strain_all[q].astype(f32)
         for c in range(cols):
             u_re = wide_re[pl.ds(c, n_k, stride=cols), :]
             u_im = wide_im[pl.ds(c, n_k, stride=cols), :]
             parts = []
             for s in range(segs):
-                d_row = strain_all[q, c * segs + s:c * segs + s + 1, :]
-                d_re, d_im = d_row[:, :half], d_row[:, half:]
+                row = c * segs + s
+                d_re, d_im = strain_q[row:row + 1, :half], strain_q[row:row + 1, half:]
                 parts.append(jnp.concatenate([u_re * d_re + u_im * d_im, u_re * d_im - u_im * d_re], axis=1))
             high, low = split(jnp.concatenate(parts, axis=0))
             out = lax.dot_general(left_hi[...], high, NT, preferred_element_type=f32)
@@ -267,65 +277,68 @@
             swap_s(off, q).wait()
 
 
-def rebuild_kernel(segs, got_ref, table_ref, rows_ref, second_hi, second_lo, out_ref,
-                   series, left_re, left_im, stage, out_sem):
+def rebuild_kernel(segs, got_ref, table_ref, rows_ref, second_hi, second_lo, out_ref, series, left, stage, out_sem):
     n, _, res, cols, wide = got_ref.shape
     side = n * cols
     n_k = wide // segs
-    step_s = pl.program_id(0)
-    step_j = pl.program_id(1)
-    j_steps = pl.num_programs(1)
-    j_block = out_ref.shape[1] // res // j_steps
-    step = step_s * j_steps + step_j
+    templates = rows_ref.shape[1]
+    tile = stage.shape[2] // templates
+    batch = tile // 2
+    step_a, step_s = pl.program_id(0), pl.program_id(1)
+    step = step_a * segs + step_s
     slot = lax.rem(step, 2)
 
-    def writes(at_slot, at_s, at_j):
-        height = j_block * res
-        span = pl.ds(pl.multiple_of(at_j * height, height), height)
-        return [pltpu.make_async_copy(stage.at[at_slot, h], out_ref.at[at_s, span, pl.ds(h * 128, 128)],
+    def writes(at_slot, at_a, at_s):
+        span = pl.ds(pl.multiple_of(at_a * tile, tile), tile)
+        return [pltpu.make_async_copy(stage.at[at_slot, h].reshape(templates, tile, 128),
+                                      out_ref.at[at_s, :, span, pl.ds(h * 128, 128)],
                                       out_sem.at[at_slot, h]) for h in range(side // 128)]
 
-    @pl.when((step_s == 0) & (step_j == 0))
+    def second(first):
+        both = []
+        for part in range(2):
+            block = jnp.concatenate([got_ref[:, part, first + i].reshape(side, wide) for i in range(batch)], axis=1)
+            both.append(lax.dot_general(block, second_hi[...], TN, preferred_element_type=f32)
+                        + lax.dot_general(block, second_lo[...], TN, preferred_element_type=f32))
+        z_re = (both[0][:, :side] - both[1][:, side:]).astype(bf16)
+        z_im = (both[0][:, side:] + both[1][:, :side]).astype(bf16)
+        for i in range(batch):
+            for s in range(segs):
+                rows = slice(i * wide + s * n_k, i * wide + (s + 1) * n_k)
+                series[s, first + i, :n_k] = z_re[rows]
+                series[s, first + i, n_k:] = z_im[rows]
+
+    @pl.when(step == 0)
     def _():
-        n_rows = table_ref.shape[0]
-        index = lax.broadcasted_iota(jnp.int32, (n_rows, rows_ref.shape[1]), 0)
+        index = lax.broadcasted_iota(jnp.int32, (table_ref.shape[0], templates), 0)
         hot = jnp.where(index == rows_ref[...], 1.0, 0.0).astype(bf16)
-        left = lax.dot_general(hot, table_ref[...], TN, preferred_element_type=f32).astype(bf16)
-        left_re[...] = left[:, :2 * n_k]
-        left_im[...] = left[:, 2 * n_k:]
-
-        @pl.loop(0, res)
-        def _(a):
-            both = []
-            for part in range(2):
-                block = got_ref[:, part, a].reshape(side, wide)
-                both.append(lax.dot_general(block, second_hi[...], TN, preferred_element_type=f32)
-                            + lax.dot_general(block, second_lo[...], TN, preferred_element_type=f32))
-            z_re = (both[0][:, :side] - both[1][:, side:]).astype(bf16)
-            z_im = (both[0][:, side:] + both[1][:, :side]).astype(bf16)
-            for s in range(segs):
-                series[s, a, :n_k] = z_re[s * n_k:(s + 1) * n_k]
-                series[s, a, n_k:] = z_im[s * n_k:(s + 1) * n_k]
+        picked = lax.dot_general(hot, table_ref[...], TN, preferred_element_type=f32).astype(bf16)
+        left[:templates] = picked[:, :2 * n_k]
+        left[templates:] = picked[:, 2 * n_k:]
+
+        @pl.loop(0, 2)
+        def _(i):
+            second(i * batch)
+
+    @pl.when((step_s < 2) & (step_a < pl.num_programs(0) - 1))
+    def _():
+        second((step_a + 1) * tile + step_s * batch)
 
     @pl.when(step >= 2)
     def _():
         for copy in writes(slot, 0, 0):
             copy.wait()
 
-    rows = pl.ds(pl.multiple_of(step_j * j_block, j_block), j_block)
-    l_re = left_re[rows, :]
-    l_im = left_im[rows, :]
-    for a in range(res):
-        right = series[step_s, a]
-        p_re = jnp.dot(l_re, right, preferred_element_type=f32)
-        p_im = jnp.dot(l_im, right, preferred_element_type=f32)
+    for a in range(tile):
+        rho = jnp.dot(left[...], series[step_s, step_a * tile + a], preferred_element_type=f32)
+        p_re, p_im = rho[:templates], rho[templates:]
         power = p_re * p_re + p_im * p_im
         for h in range(side // 128):
-            stage[slot, h, pl.ds(a, j_block, stride=res), :] = power[:, h * 128:(h + 1) * 128]
-    for copy in writes(slot, step_s, step_j):
+            stage[slot, h, pl.ds(a, templates, stride=tile), :] = power[:, h * 128:(h + 1) * 128]
+    for copy in writes(slot, step_a, step_s):
         copy.start()
 
-    @pl.when(step == pl.num_programs(0) * j_steps - 1)
+    @pl.when(step == pl.num_programs(0) * segs - 1)
     def _():
         for at_slot in range(2):
             for copy in writes(at_slot, 0, 0):
@@ -340,7 +353,7 @@
     res = side // n
     templates = template_rows.shape[0]
     wide = segs * n_k
-    if cols % 16 or wide != 128 or n_k % 16 or coefficients.shape[0] % 16 or math.isqrt(n) ** 2 != n:
+    if cols % 16 or segs < 2 or wide != 128 or n_k % 16 or coefficients.shape[0] % 16 or math.isqrt(n) ** 2 != n:
         return shards_general(strain, basis_vectors, coefficients, template_rows)
     samples = side * side
     cos1, sin1 = table(side, half, side)
@@ -360,7 +373,7 @@
     packed_coeff = jnp.concatenate([c_re, -c_im, c_im, c_re], axis=1)
     rows_loc = coefficients.shape[0]
     u = basis_vectors.reshape(k_loc, side, side)
-    d = strain.reshape(cols * segs, side)
+    d = strain.astype(bf16).reshape(cols * segs, side)
     vmem = pl.BlockSpec(memory_space=pltpu.VMEM)
     hbm = pl.BlockSpec(memory_space=pl.ANY)
     got, coeff_table = pl.pallas_call(
@@ -371,7 +384,7 @@
         out_specs=[hbm, hbm],
         scratch_shapes=[
             pltpu.VMEM((layers, layers, group, k_loc, cols, side), bf16),
-            pltpu.VMEM((layers, cols * segs, side), f32),
+            pltpu.VMEM((layers, cols * segs, side), bf16),
             pltpu.VMEM((n_k * cols, half), f32),
             pltpu.VMEM((n_k * cols, half), f32),
             pltpu.VMEM((2, group * res * cols, wide), f32),
@@ -383,22 +396,20 @@
             (n,), (n,), (group, layers), (group, layers), (3, layers))],
         compiler_params=pltpu.CompilerParams(collective_id=0, has_side_effects=True),
     )(u, d, packed_coeff, first_hi, first_lo, turn)
-    j_block = templates // 2
-    power = pl.pallas_call(
+    tile = 8
+    return pl.pallas_call(
         functools.partial(rebuild_kernel, segs),
-        grid=(segs, templates // j_block),
-        out_shape=jax.ShapeDtypeStruct((segs, templates * res, side), f32),
+        grid=(res // tile, segs),
+        out_shape=jax.ShapeDtypeStruct((segs, templates, res, side), f32),
         in_specs=[vmem] * 5,
         out_specs=hbm,
         scratch_shapes=[
             pltpu.VMEM((segs, res, 2 * n_k, side), bf16),
-            pltpu.VMEM((templates, 2 * n_k), bf16),
-            pltpu.VMEM((templates, 2 * n_k), bf16),
-            pltpu.VMEM((2, side // 128, j_block * res, 128), f32),
+            pltpu.VMEM((2 * templates, 2 * n_k), bf16),
+            pltpu.VMEM((2, side // 128, templates * tile, 128), f32),
             pltpu.SemaphoreType.DMA((2, side // 128)),
         ],
     )(got, coeff_table.reshape(n * rows_loc, 4 * n_k), template_rows[None], second_hi, second_lo)
-    return power.reshape(segs, templates, res, side)
 
 
 def solution(mesh):

time: 74.1 us -> 69.9 us (0.943)
  Pallas kernels: 67.6 us -> 63.5 us
  other arithmetic: 2 us -> 2.88 us
  local copies, waits for them, and re-layouts: 4.11 us -> 3.25 us
    pallas_call x1, Pallas kernels: 19.5 us -> 14 us  [shards(): pl.pallas_call(functools.partial(rebuild_kernel, segs), grid=(res // tile...]
    pallas_call x1, Pallas kernels: 48.2 us -> 49.5 us  [shards(): pl.pallas_call(functools.partial(exchange, n, group, segs), out_shape=[ja...]
    convert_element_type x0 -> x1, other arithmetic: none -> 0.87 us  [shards(): d = strain.astype(bf16).reshape(cols * segs, side)]
    unnamed x2, local copies, waits for them, and re-layouts: 2.2 us -> 1.34 us
where the time goes in v2:
time: 69.9 us; the launch traced here: 69.6 us
  Pallas kernels  63.5 us (91%)
  local copies, waits for them, and re-layouts  3.25 us (5%)
  other arithmetic  2.88 us (4%)
    pallas_call x1, Pallas kernels, shards(): pl.pallas_call(functools.partial(exchange, n, group, segs), out_shape=[ja...  49.5 us
    pallas_call x1, Pallas kernels, shards(): pl.pallas_call(functools.partial(rebuild_kernel, segs), grid=(res // tile...  14 us
    reshape x1, local copies, waits for them, and re-layouts, shards(): u = basis_vectors.reshape(k_loc, side, side)  1.82 us

profile of v2, /device:TPU:1, one launch (start us, length us, event | category | flops | bytes accessed | tf_op | source)
XLA Modules:
  0.0 69.6 jit_solution(14785839607296817640)
XLA Ops:
  0.0 0.7 %copy.15 = bf16[16,2,32]{2,0,1:T(8,128)(2,1)S(1)} copy(f32[16,2,32]{2,1,0:T(2,128)} %param.10) | data formatting | bytes 6144 | tf_op args[2]
  0.7 0.7 pad_maximum_fusion.1.coeff_ref
  1.4 0.1 fusion.1
  1.5 0.9 %convert_element_type.14 = bf16[16,4,2,128]{3,2,1,0:T(2,128)(2,1)S(1)} convert(f32[16,4,2,128]{3,2,1,0:T(2,128)} %param.8) | non-fusion elementwise | flops 16384 | bytes 98304 | tf_op jit(solution)/shard_map/convert_element_type | solution.py:376
  2.4 0.6 copy.16
  3.0 0.1 copy.11
  3.1 0.5 multiply_cosine_fusion
  3.6 0.8 %pad_maximum_fusion.turn_ref = f32[4,64,32]{2,1,0:T(8,128)} fusion(f32[4,64,16]{2,1,0:T(8,128)S(1)} %get-tuple-element.10, f32[4,64,16]{2,1,0:T(8,128)S(1)} %get-tuple-element.9), kind=kLoop, calls=%fused_computation | loop fusion | flops 8192 | bytes 65536 | tf_op jit(solution)/shard_map/concatenate | solution.py:371
  4.3 1.8 %reshape.11.u_ref = bf16[2,256,256]{2,1,0:T(8,128)(2,1)} reshape(bf16[2,256,2,128]{3,2,1,0:T(2,128)(2,1)} %param.9) | data formatting | bytes 524288 | tf_op jit(solution)/shard_map/reshape | solution.py:375
  6.2 49.5 %shard_map.82 = (bf16[16,2,16,16,128]{4,3,2,1,0:T(8,128)(2,1)}, bf16[16,16,128]{2,1,0:T(8,128)(2,1)}) custom-call(bf16[2,256,256]{2,1,0:T(8,128)(2,1)} %reshape.11.u_ref, bf16[64,256]{1,0:T(8,128)(2,1)} %bitcast.14, bf16[16,128]{1,0:T(8,128)(2,1)} %pad_maximum_fusion.1.coeff_ref, bf16[512,256]{1,0:T(8,128)(2,1)} %constant.60.clone.first_hi, ...), custom_call_target="tpu_custom_call" | custom-call | tf_op jit(solution)/shard_map/pallas_call | solution.py:379
  55.6 14.0 %shard_map.83 = f32[4,256,16,256]{3,2,1,0:T(8,128)} custom-call(bf16[16,2,16,16,128]{4,3,2,1,0:T(8,128)(2,1)} %get-tuple-element.7.got_ref, bf16[256,128]{1,0:T(8,128)(2,1)} %bitcast.15, s32[1,256]{1,0:T(1,128)} %bitcast.16, bf16[256,512]{1,0:T(8,128)(2,1)} %constant.62.clone.second_hi, bf16[256,512]{1,0:T(8,128)(2,1)} %constant.63.clone.second_lo), custom_call_target="tpu_custom_call" | custom-call | tf_op jit(solution)/shard_map/pallas_call | solution.py:400
  (4 shorter events, 0.0 us)

commit v3 on v2

--- a/solution.py
+++ b/solution.py
@@ -159,18 +159,25 @@
     def towards(way):
         return layer < layers - 1 if way else layer > 0
 
-    def relay(copy_of):
-        for dist in range(1, layers):
-            for way in range(2):
-                origin = layer - dist if way else layer + dist
-
-                @pl.when((origin >= 0) & (origin < layers))
+    def relay(q, dist):
+        for way in range(2):
+            origin = layer - dist if way else layer + dist
+
+            @pl.when((origin >= 0) & (origin < layers))
+            def _():
+                @pl.when(origin == q)
                 def _():
-                    copy_of(origin, 0).wait_recv()
+                    pass_d(origin, 0).wait_recv()
 
                     @pl.when(towards(way))
                     def _():
-                        copy_of(origin, way).start()
+                        pass_d(origin, way).start()
+
+                pass_u(q, origin, 0).wait_recv()
+
+                @pl.when(towards(way))
+                def _():
+                    pass_u(q, origin, way).start()
 
     def drain(copy_of):
         for origin in range(layers):
@@ -214,27 +221,22 @@
         left_hi[part * near:(part + 1) * near, :] = first_hi[rows, :]
         left_lo[part * near:(part + 1) * near, :] = first_lo[rows, :]
     launch(0)
+    launch(1)
+    for stage in range(1, layers - 1):
+        for dist in range(1, stage + 1):
+            relay(stage - dist, dist)
+        launch(stage + 1)
     for off in range(1, n):
         share_c(off).start()
-    launch(1)
 
     @pl.loop(0, layers)
     def _(q):
-        @pl.when(layer != q)
-        def _():
-            pass_d(q, 0).wait_recv()
-            for way in range(2):
-                ahead = layer > q if way else layer < q
-
-                @pl.when(towards(way) & ahead)
-                def _():
-                    pass_d(q, way).start()
-
-        relay(functools.partial(pass_u, q))
-
-        @pl.when(q + 2 < layers)
-        def _():
-            launch(q + 2)
+        for dist in range(1, layers):
+            chunk = q + layers - 1 - dist
+
+            @pl.when(chunk < layers)
+            def _():
+                relay(chunk, dist)
 
         wide = u_all[q].astype(f32).reshape(n_k * cols, side)
         wide_re[...] = wide[:, :half]

time: 69.9 us -> 68.3 us (0.977)
  Pallas kernels: 63.5 us -> 61.8 us
    pallas_call x1, Pallas kernels: 49.5 us -> 47.8 us  [shards(): pl.pallas_call(functools.partial(exchange, n, group, segs), out_shape=[ja...]
where the time goes in v3:
time: 68.3 us; the launch traced here: 68 us
  Pallas kernels  61.8 us (90%)
  local copies, waits for them, and re-layouts  3.25 us (5%)
  other arithmetic  2.88 us (4%)
    pallas_call x1, Pallas kernels, shards(): pl.pallas_call(functools.partial(exchange, n, group, segs), out_shape=[ja...  47.8 us
    pallas_call x1, Pallas kernels, shards(): pl.pallas_call(functools.partial(rebuild_kernel, segs), grid=(res // tile...  14 us
    reshape x1, local copies, waits for them, and re-layouts, shards(): u = basis_vectors.reshape(k_loc, side, side)  1.82 us

profile of v3, /device:TPU:1, one launch (start us, length us, event | category | flops | bytes accessed | tf_op | source)
XLA Modules:
  0.0 68.0 jit_solution(6719134056267583799)
XLA Ops:
  0.0 0.7 %copy.15 = bf16[16,2,32]{2,0,1:T(8,128)(2,1)S(1)} copy(f32[16,2,32]{2,1,0:T(2,128)} %param.10) | data formatting | bytes 6144 | tf_op args[2]
  0.7 0.7 pad_maximum_fusion.1.coeff_ref
  1.4 0.1 fusion.1
  1.5 0.9 %convert_element_type.14 = bf16[16,4,2,128]{3,2,1,0:T(2,128)(2,1)S(1)} convert(f32[16,4,2,128]{3,2,1,0:T(2,128)} %param.8) | non-fusion elementwise | flops 16384 | bytes 98304 | tf_op jit(solution)/shard_map/convert_element_type | solution.py:378
  2.4 0.6 copy.16
  3.0 0.1 copy.11
  3.1 0.5 multiply_cosine_fusion
  3.6 0.8 %pad_maximum_fusion.turn_ref = f32[4,64,32]{2,1,0:T(8,128)} fusion(f32[4,64,16]{2,1,0:T(8,128)S(1)} %get-tuple-element.10, f32[4,64,16]{2,1,0:T(8,128)S(1)} %get-tuple-element.9), kind=kLoop, calls=%fused_computation | loop fusion | flops 8192 | bytes 65536 | tf_op jit(solution)/shard_map/concatenate | solution.py:373
  4.3 1.8 %reshape.11.u_ref = bf16[2,256,256]{2,1,0:T(8,128)(2,1)} reshape(bf16[2,256,2,128]{3,2,1,0:T(2,128)(2,1)} %param.9) | data formatting | bytes 524288 | tf_op jit(solution)/shard_map/reshape | solution.py:377
  6.2 47.8 %shard_map.82 = (bf16[16,2,16,16,128]{4,3,2,1,0:T(8,128)(2,1)}, bf16[16,16,128]{2,1,0:T(8,128)(2,1)}) custom-call(bf16[2,256,256]{2,1,0:T(8,128)(2,1)} %reshape.11.u_ref, bf16[64,256]{1,0:T(8,128)(2,1)} %bitcast.14, bf16[16,128]{1,0:T(8,128)(2,1)} %pad_maximum_fusion.1.coeff_ref, bf16[512,256]{1,0:T(8,128)(2,1)} %constant.60.clone.first_hi, ...), custom_call_target="tpu_custom_call" | custom-call | tf_op jit(solution)/shard_map/pallas_call | solution.py:381
  54.0 14.0 %shard_map.83 = f32[4,256,16,256]{3,2,1,0:T(8,128)} custom-call(bf16[16,2,16,16,128]{4,3,2,1,0:T(8,128)(2,1)} %get-tuple-element.7.got_ref, bf16[256,128]{1,0:T(8,128)(2,1)} %bitcast.15, s32[1,256]{1,0:T(1,128)} %bitcast.16, bf16[256,512]{1,0:T(8,128)(2,1)} %constant.62.clone.second_hi, bf16[256,512]{1,0:T(8,128)(2,1)} %constant.63.clone.second_lo), custom_call_target="tpu_custom_call" | custom-call | tf_op jit(solution)/shard_map/pallas_call | solution.py:402
  (4 shorter events, 0.0 us)

commit v4 on v3

--- a/solution.py
+++ b/solution.py
@@ -103,14 +103,14 @@
     return high, (values - high.astype(np.float32)).astype(bf16)
 
 
-def exchange(n, group, segs, u_ref, strain_ref, coeff_ref, first_hi, first_lo, turn_ref, got_ref, table_ref,
-             u_all, strain_all, wide_re, wide_im, sect, packed, left_hi, left_lo,
+def exchange(n, group, segs, u_ref, strain_ref, coeff_ref, first_hi, first_lo, got_ref, table_ref,
+             u_all, strain_all, wide, sect, packed, left_hi, left_lo,
              send_u, recv_u, send_z, recv_z, send_d, recv_d, send_c, recv_c, send_s, recv_s, own_sem):
     me = lax.axis_index("basis")
     layers = n // group
     layer = me // group
     lane = lax.rem(me, group)
-    k_loc, side = u_ref.shape[0], u_ref.shape[1]
+    k_loc, side = u_ref.shape[0], u_ref.shape[1] // 2
     cols = side // n
     half = side // 2
     n_k = k_loc * n
@@ -125,7 +125,7 @@
         return lax.rem(lane + off, group)
 
     def columns(q, owner):
-        return pl.ds(pl.multiple_of((q * group + owner) * cols, cols), cols)
+        return pl.ds(pl.multiple_of((q * group + owner) * 2 * cols, 2 * cols), 2 * cols)
 
     def swap_u(off, q):
         to = mate(off)
@@ -205,13 +205,11 @@
     for off in range(1, n):
         pl.semaphore_signal(barrier, inc=1, device_id={"basis": lax.rem(me + off, n)},
                             device_id_type=pl.DeviceIdType.MESH)
-    own_d = pltpu.make_async_copy(strain_ref, strain_all.at[layer], own_sem.at[2, 0])
-    own_d.start()
-    own_c = pltpu.make_async_copy(coeff_ref, table_ref.at[me], own_sem.at[2, 1])
+    strain_all[layer] = strain_ref[...].astype(bf16)
+    own_c = pltpu.make_async_copy(coeff_ref, table_ref.at[me], own_sem.at[2, 0])
     own_c.start()
     for q in range(layers):
         keep_u(q).start()
-    own_d.wait()
     pl.semaphore_wait(barrier, n - 1)
     for q in range(layers):
         for off in range(1, group):
@@ -238,25 +236,26 @@
             def _():
                 relay(chunk, dist)
 
-        wide = u_all[q].astype(f32).reshape(n_k * cols, side)
-        wide_re[...] = wide[:, :half]
-        wide_im[...] = wide[:, half:]
-        turn = turn_ref[q]
+        wide[...] = u_all[q].astype(f32).reshape(wide.shape)
+        column = (q * group + lane) * cols + lax.broadcasted_iota(jnp.int32, (near, cols), 1)
+        residue = layer * near + lax.broadcasted_iota(jnp.int32, (near, cols), 0)
+        angle = lax.rem(column * residue, side * side).astype(f32) * (2.0 * math.pi / (side * side))
+        turn_cos, turn_sin = jnp.cos(angle), jnp.sin(angle)
         strain_q = strain_all[q].astype(f32)
         for c in range(cols):
-            u_re = wide_re[pl.ds(c, n_k, stride=cols), :]
-            u_im = wide_im[pl.ds(c, n_k, stride=cols), :]
+            u_re = wide[pl.ds(2 * c, n_k, stride=2 * cols), :]
+            u_im = wide[pl.ds(2 * c + 1, n_k, stride=2 * cols), :]
             parts = []
             for s in range(segs):
-                row = c * segs + s
-                d_re, d_im = strain_q[row:row + 1, :half], strain_q[row:row + 1, half:]
+                row = 2 * (c * segs + s)
+                d_re, d_im = strain_q[row:row + 1], strain_q[row + 1:row + 2]
                 parts.append(jnp.concatenate([u_re * d_re + u_im * d_im, u_re * d_im - u_im * d_re], axis=1))
             high, low = split(jnp.concatenate(parts, axis=0))
             out = lax.dot_general(left_hi[...], high, NT, preferred_element_type=f32)
             out += lax.dot_general(left_lo[...], high, NT, preferred_element_type=f32)
             out += lax.dot_general(left_hi[...], low, NT, preferred_element_type=f32)
-            t_cos = turn[:, c:c + 1]
-            t_sin = turn[:, cols + c:cols + c + 1]
+            t_cos = turn_cos[:, c:c + 1]
+            t_sin = turn_sin[:, c:c + 1]
             o_re, o_im = out[:near], out[near:]
             sect[0, pl.ds(c, near, stride=cols), :] = o_re * t_cos - o_im * t_sin
             sect[1, pl.ds(c, near, stride=cols), :] = o_re * t_sin + o_im * t_cos
@@ -357,7 +356,6 @@
     wide = segs * n_k
     if cols % 16 or segs < 2 or wide != 128 or n_k % 16 or coefficients.shape[0] % 16 or math.isqrt(n) ** 2 != n:
         return shards_general(strain, basis_vectors, coefficients, template_rows)
-    samples = side * side
     cos1, sin1 = table(side, half, side)
     first_hi, first_lo = halves(np.block([[cos1, -sin1], [sin1, cos1]]))
     cos2, sin2 = table(side, side, side)
@@ -365,30 +363,23 @@
     me = lax.axis_index("basis")
     group = math.isqrt(n)
     layers = n // group
-    grid = (layers, group * res, cols)
-    lane = me % group
-    column = (lax.broadcasted_iota(jnp.int32, grid, 0) * group + lane) * cols + lax.broadcasted_iota(jnp.int32, grid, 2)
-    residue = me // group * group * res + lax.broadcasted_iota(jnp.int32, grid, 1)
-    angle = (column * residue % samples).astype(f32) * (2.0 * math.pi / samples)
-    turn = jnp.concatenate([jnp.cos(angle), jnp.sin(angle)], axis=2)
     c_re, c_im = coefficients[:, 0].astype(bf16), coefficients[:, 1].astype(bf16)
     packed_coeff = jnp.concatenate([c_re, -c_im, c_im, c_re], axis=1)
     rows_loc = coefficients.shape[0]
-    u = basis_vectors.reshape(k_loc, side, side)
-    d = strain.astype(bf16).reshape(cols * segs, side)
+    u = basis_vectors.reshape(k_loc, 2 * side, half)
+    d = strain.reshape(2 * cols * segs, half)
     vmem = pl.BlockSpec(memory_space=pltpu.VMEM)
     hbm = pl.BlockSpec(memory_space=pl.ANY)
     got, coeff_table = pl.pallas_call(
         functools.partial(exchange, n, group, segs),
         out_shape=[jax.ShapeDtypeStruct((n, 2, res, cols, wide), bf16),
                    jax.ShapeDtypeStruct((n, rows_loc, 4 * n_k), bf16)],
-        in_specs=[vmem] * 6,
+        in_specs=[vmem] * 5,
         out_specs=[hbm, hbm],
         scratch_shapes=[
-            pltpu.VMEM((layers, layers, group, k_loc, cols, side), bf16),
-            pltpu.VMEM((layers, cols * segs, side), bf16),
-            pltpu.VMEM((n_k * cols, half), f32),
-            pltpu.VMEM((n_k * cols, half), f32),
+            pltpu.VMEM((layers, layers, group, k_loc, 2 * cols, half), bf16),
+            pltpu.VMEM((layers, 2 * cols * segs, half), bf16),
+            pltpu.VMEM((2 * n_k * cols, half), f32),
             pltpu.VMEM((2, group * res * cols, wide), f32),
             pltpu.VMEM((layers, 2, group * res, cols, wide), bf16),
             pltpu.VMEM((2 * group * res, side), bf16),
@@ -397,7 +388,7 @@
             (group, layers), (group, layers), (layers, layers, 2), (layers, layers), (layers, 2), (layers,),
             (n,), (n,), (group, layers), (group, layers), (3, layers))],
         compiler_params=pltpu.CompilerParams(collective_id=0, has_side_effects=True),
-    )(u, d, packed_coeff, first_hi, first_lo, turn)
+    )(u, d, packed_coeff, first_hi, first_lo)
     tile = 8
     return pl.pallas_call(
         functools.partial(rebuild_kernel, segs),

time: 68.3 us -> 63.7 us (0.933)
  local copies, waits for them, and re-layouts: 3.25 us -> 0.72 us
  other arithmetic: 2.88 us -> 0.68 us
    reshape x1 -> x0, local copies, waits for them, and re-layouts: 1.82 us -> none  [shards(): u = basis_vectors.reshape(k_loc, side, side)]
    convert_element_type x2 -> x0, other arithmetic: 0.95 us -> none  [the longest x1 0.87 us: shards(): d = strain.astype(bf16).reshape(cols * segs, side)]
    concatenate x1 -> x0, other arithmetic: 0.77 us -> none  [shards(): turn = jnp.concatenate([jnp.cos(angle), jnp.sin(angle)], axis=2)]
where the time goes in v4:
time: 63.7 us; the launch traced here: 63.5 us
  Pallas kernels  62.1 us (97%)
  local copies, waits for them, and re-layouts  0.72 us (1%)
  other arithmetic  0.68 us (1%)
    pallas_call x1, Pallas kernels, shards(): pl.pallas_call(functools.partial(exchange, n, group, segs), out_shape=[ja...  48.1 us
    pallas_call x1, Pallas kernels, shards(): pl.pallas_call(functools.partial(rebuild_kernel, segs), grid=(res // tile...  14 us

profile of v4, /device:TPU:1, one launch (start us, length us, event | category | flops | bytes accessed | tf_op | source)
XLA Modules:
  0.0 63.5 jit_solution(3180443079099088070)
XLA Ops:
  0.0 0.7 %copy.11 = bf16[16,2,32]{2,0,1:T(8,128)(2,1)S(1)} copy(f32[16,2,32]{2,1,0:T(2,128)} %param.10) | data formatting | bytes 6144 | tf_op args[2]
  0.7 0.7 %pad_maximum_fusion.coeff_ref = bf16[16,128]{1,0:T(8,128)(2,1)} fusion(bf16[16,32]{1,0:T(8,128)(2,1)S(1)} %get-tuple-element.10, bf16[16,32]{1,0:T(8,128)(2,1)S(1)} %get-tuple-element.9, bf16[16,32]{1,0:T(8,128)(2,1)S(1)} %fusion), kind=kLoop, calls=%fused_computation.3 | loop fusion | flops 16384 | bytes 7168 | tf_op jit(solution)/shard_map/concatenate | solution.py:367
  1.4 48.1 %shard_map.82 = (bf16[16,2,16,16,128]{4,3,2,1,0:T(8,128)(2,1)}, bf16[16,16,128]{2,1,0:T(8,128)(2,1)}) custom-call(bf16[2,512,128]{2,1,0:T(8,128)(2,1)} %bitcast.10, f32[128,128]{1,0:T(8,128)} %bitcast.12, bf16[16,128]{1,0:T(8,128)(2,1)} %pad_maximum_fusion.coeff_ref, bf16[512,256]{1,0:T(8,128)(2,1)} %constant.8.clone.first_hi, ...), custom_call_target="tpu_custom_call" | custom-call | tf_op jit(solution)/shard_map/pallas_call | solution.py:373
  49.5 14.0 %shard_map.83 = f32[4,256,16,256]{3,2,1,0:T(8,128)} custom-call(bf16[16,2,16,16,128]{4,3,2,1,0:T(8,128)(2,1)} %get-tuple-element.7.got_ref, bf16[256,128]{1,0:T(8,128)(2,1)} %bitcast.11, s32[1,256]{1,0:T(1,128)} %bitcast.13, bf16[256,512]{1,0:T(8,128)(2,1)} %constant.10.clone.second_hi, bf16[256,512]{1,0:T(8,128)(2,1)} %constant.11.clone.second_lo), custom_call_target="tpu_custom_call" | custom-call | tf_op jit(solution)/shard_map/pallas_call | solution.py:393
  (2 shorter events, 0.0 us)
